TPU v7x, 32 devices: a whole 2x2x4 slice. The times are simulated.
32 devices in a mesh: member: 4 (over x, core), gx: 2 (over y), gy: 4 (over z).
Axes of the slice: x: 2, y: 2, z: 4, core: 2. Of those that a mesh axis runs over, the one named last changes fastest.
Arguments:
- tracers: float32 [8, 16, 128, 512], P('member', None, 'gx', 'gy'), may hold values from -6 to 6
- flux_x: float32 [16, 128, 512], P('member', 'gx', 'gy'), may hold values from -0.4 to 0.4
- flux_y: float32 [16, 128, 512], P('member', 'gx', 'gy'), may hold values from -0.4 to 0.4
- flux_z: float32 [16, 128, 512], P('member', 'gx', 'gy'), may hold values from -0.4 to 0.4
Outputs:
- transported: float32 [8, 16, 128, 512], P('member', None, 'gx', 'gy')
All inputs are finite; a program needn't handle non-finite values.
Results may differ from a plain program's by a relative error of at most 0.0003.
Values sent between devices are 32-bit elements; how exact they have to be, the bound alone decides.
A program may use at most 128 MiB of HBM per device.

v0:
```python
import jax
import jax.numpy as jnp
from jax import lax
from jax.sharding import PartitionSpec as P


def extended_2(block, sides, width):
    for axis, dim in sides:
        count = lax.axis_size(axis)
        forward = [(i, i + 1) for i in range(count - 1)]
        forward.append((count - 1, 0))
        backward = [(target, source) for source, target in forward]
        low = lax.ppermute(
            lax.slice_in_dim(block, block.shape[dim] - width, None, axis=dim), axis, forward
        )
        high = lax.ppermute(lax.slice_in_dim(block, 0, width, axis=dim), axis, backward)
        block = jnp.concatenate([low, block, high], axis=dim)
    return block


def advect(field, faces, axis):
    faces = jnp.reshape(faces, (1,) * (field.ndim - faces.ndim) + faces.shape)
    cells = faces.shape[axis] - 1

    def along(source, start, stop):
        return lax.slice_in_dim(source, start, stop, axis=axis)

    face_values = (
        7.0 * (along(field, 1, cells + 4) + along(field, 2, cells + 5))
        - (along(field, 0, cells + 3) + along(field, 3, cells + 6))
    ) / 12.0
    lower_a = along(face_values, 0, cells + 1)
    lower_b = along(face_values, 1, cells + 2)
    lower_mid = along(field, 2, cells + 3)
    upper_b = along(face_values, 2, cells + 3)
    upper_mid = along(field, 3, cells + 4)
    lower_d = lower_b - lower_a
    lower_h = 6.0 * lower_mid - 3.0 * (lower_a + lower_b)
    upper_d = upper_b - lower_b
    upper_h = 6.0 * upper_mid - 3.0 * (lower_b + upper_b)
    gauge = -faces
    from_lower = faces * (lower_b - 0.5 * faces * (lower_d - (1.0 - 2.0 * faces / 3.0) * lower_h))
    from_upper = faces * (lower_b + 0.5 * gauge * (upper_d + (1.0 - 2.0 * gauge / 3.0) * upper_h))
    face_flux = jnp.where(faces > 0, from_lower, from_upper)
    return along(field, 3, cells + 3) - (
        along(face_flux, 1, cells + 1) - along(face_flux, 0, cells)
    )


def vertical(field, lower_faces):
    padded = jnp.concatenate(
        [
            field[:, :1],
            field[:, :1],
            field[:, :1],
            field,
            field[:, -1:],
            field[:, -1:],
            field[:, -1:],
        ],
        axis=1,
    )
    closed = jnp.zeros_like(lower_faces[:1])
    faces = jnp.concatenate([closed, lower_faces[:-1], closed], axis=0)
    return advect(padded, faces, 1)


def cut_faces(winds, wind_rim, rim_x, rim_y, width_x, width_y):
    wind_x, wind_y, wind_z = winds
    face_x = wind_x[
        :,
        wind_rim - rim_x - 1 : wind_rim + width_x + rim_x,
        wind_rim - rim_y : wind_rim + width_y + rim_y,
    ]
    face_y = wind_y[
        :,
        wind_rim - rim_x : wind_rim + width_x + rim_x,
        wind_rim - rim_y + 2 : wind_rim + width_y + rim_y - 3,
    ]
    face_z = wind_z[
        :,
        wind_rim - rim_x : wind_rim + width_x + rim_x,
        wind_rim - rim_y + 3 : wind_rim + width_y + rim_y - 3,
    ]
    return (face_x, face_y, face_z)


def advance(field, winds, rim, width_x, width_y):
    wind_rim = (winds[0].shape[1] - width_x) // 2
    face_x, face_y, face_z = cut_faces(winds, wind_rim, rim - 3, rim, width_x, width_y)
    field = advect(field, face_x, 2)
    field = advect(field, face_y, 3)
    field = vertical(field, face_z)
    return field


def wind_rims(stacked):
    return extended_2(stacked, (("gx", 1), ("gy", 2)), 4)


def gathered(stacked):
    return lax.all_gather(stacked, "member", axis=0, tiled=True)


def split_winds(whole, members, slab):
    shaped = jnp.reshape(whole, (members, 3, slab) + whole.shape[1:])
    return (
        shaped[:, 0].reshape((members * slab,) + whole.shape[1:]),
        shaped[:, 1].reshape((members * slab,) + whole.shape[1:]),
        shaped[:, 2].reshape((members * slab,) + whole.shape[1:]),
    )


def body(tracers, flux_x, flux_y, flux_z):
    width_x = tracers.shape[2]
    width_y = tracers.shape[3]
    members = lax.axis_size("member")
    slab = flux_x.shape[0]
    stacked = jnp.concatenate([flux_x, flux_y, flux_z], axis=0)
    whole = wind_rims(gathered(stacked))
    winds = split_winds(whole, members, slab)
    field = tracers
    for step_index in range(2):
        extended = extended_2(field, (("gx", 2), ("gy", 3)), 3)
        field = advance(extended, winds, 3, width_x, width_y)
    return field


def solution(mesh):
    return jax.shard_map(
        body,
        mesh=mesh,
        in_specs=(
            P("member", None, "gx", "gy"),
            P("member", "gx", "gy"),
            P("member", "gx", "gy"),
            P("member", "gx", "gy"),
        ),
        out_specs=P("member", None, "gx", "gy"),
        check_vma=False,
    )
```

profile of v0, /device:TPU:0, one launch (start us, length us, event | category | flops | bytes accessed | tf_op | source)
XLA Modules:
  0.0 164.3 jit_solution(7833414720530679951)
XLA Ops:
  9.5 3.0 %collective-permute-start = (f32[2,16,3,128]{3,1,2,0:T(8,128)S(1)}, f32[2,16,3,128]{3,1,2,0:T(8,128)S(1)}, u32[]{:S(2)}, u32[]{:S(2)}) collective-permute-start(f32[2,16,3,128]{3,1,2,0:T(8,128)S(1)} %copy.112), channel_id=1, source_target_pairs={{0,4},{4,0},{1,5},{5,1},{2,6},{6,2},{3,7},{7,3},{8,12},{12,8},{9,1... | collective-permute-start | bytes 147464 | tf_op jit(solution)/shard_map/ppermute | solution.py:13
  19.9 2.5 %collective-permute-start.2 = (f32[2,16,70,3]{2,1,3,0:T(8,128)S(1)}, f32[2,16,70,3]{2,1,3,0:T(8,128)S(1)}, u32[]{:S(2)}, u32[]{:S(2)}) collective-permute-start(f32[2,16,70,3]{2,1,3,0:T(8,128)S(1)} %get-tuple-element.7), channel_id=1, source_target_pairs={{0,1},{1,2},{2,3},{3,0},{4,5},{5,6},{6,7},{7,4},{8,9},{9,10},{10,1... | collective-permute-start | bytes 80648 | tf_op jit(solution)/shard_map/ppermute | solution.py:13
  24.5 6.8 %all-gather.2.cloned.1.call-done = f32[48,64,128]{2,1,0:T(8,128)} async-done(((f32[12,64,128]{2,1,0:T(8,128)}), f32[48,64,128]{2,1,0:T(8,128)}) %all-gather.2.cloned.1.call-update) | async-done | bytes 1572880 | tf_op jit(solution)/shard_map/all_gather | solution.py:102
  34.5 4.0 %pad_maximum_fusion.15 = f32[2,16,70,134]{2,1,3,0:T(8,128)S(1)} fusion(f32[2,16,70,3]{2,1,3,0:T(8,128)S(1)} %collective-permute-done.3, f32[2,16,3,128]{2,1,3,0:T(8,128)} %copy.94, f32[2,16,64,128]{2,1,3,0:T(8,128)} %copy-done, f32[2,16,3,128]{2,1,3,0:T(8,128)} %copy.92, f32[2,16,70,3]{2,1,3,0:T(8,128)S(1)} %collective-permute-done.2), kind=kLoop, calls=%fused_computation.103 | loop fusion | flops 1200640 | bytes 2401280 | tf_op jit(solution)/shard_map/concatenate | solution.py:17
  46.1 3.4 %collective-permute-start.7 = (f32[48,72,4]{1,0,2:T(8,128)S(1)}, f32[48,72,4]{1,0,2:T(8,128)S(1)}, u32[]{:S(2)}, u32[]{:S(2)}) collective-permute-start(f32[48,72,4]{1,0,2:T(8,128)S(1)} %copy.96), channel_id=1, source_target_pairs={{1,0},{2,1},{3,2},{0,3},{5,4},{6,5},{7,6},{4,7},{9,8},{10,9},{11,1... | collective-permute-start | bytes 165896 | tf_op jit(solution)/shard_map/ppermute | solution.py:16
  49.5 3.1 %fusion.72 = f32[2,16,67,134]{2,1,3,0:T(8,128)} fusion(f32[2,16,70,134]{2,1,3,0:T(8,128)S(1)} %pad_maximum_fusion.15), kind=kLoop, calls=%fused_computation.100 | loop fusion | flops 1436480 | bytes 5745920 | tf_op jit(solution)/shard_map/div | solution.py:28
  52.6 3.3 %collective-permute-done.6 = f32[48,72,4]{1,0,2:T(8,128)S(1)} collective-permute-done((f32[48,72,4]{1,0,2:T(8,128)S(1)}, f32[48,72,4]{1,0,2:T(8,128)S(1)}, u32[]{:S(2)}, u32[]{:S(2)}) %collective-permute-start.6) | collective-permute-done | bytes 55328 | tf_op jit(solution)/shard_map/ppermute | solution.py:13
  59.6 4.1 %pad_maximum_fusion.14 = f32[48,72,136]{2,1,0:T(8,128)S(1)} fusion(f32[48,72,4]{2,1,0:T(8,128)} %copy.98, f32[48,4,128]{2,1,0:T(4,128)S(1)} %collective-permute-done.5, f32[48,64,128]{2,1,0:T(8,128)} %all-gather.2.cloned.1.call-done, f32[48,4,128]{2,1,0:T(4,128)S(1)} %collective-permute-done.4, f32[48,72,4]{2,1,0:T(8,128)} %copy.97), kind=kLoop, calls=%fused_computation.14 | loop fusion | flops 1880064 | bytes 3760128 | tf_op jit(solution)/shard_map/concatenate | solution.py:17
  70.3 2.8 %fusion.116 = (f32[16,64,129]{1,0,2:T(8,128)}, f32[16,64,129]{1,0,2:T(8,128)}, f32[16,64,129]{1,0,2:T(8,128)}, f32[16,64,129]{1,0,2:T(8,128)}, f32[16,64,129]{1,0,2:T(8,128)}) fusion(f32[16,72,136]{1,0,2:T(8,128)S(1)} %bitcast.8), kind=kLoop, calls=%fused_computation.183 | loop fusion | flops 924672 | bytes 3170304 | tf_op jit(solution)/shard_map/slice | solution.py:75
  76.9 3.7 %fusion.117 = (f32[16,65,134]{1,0,2:T(8,128)S(1)}, f32[16,65,134]{1,0,2:T(8,128)}, f32[16,65,134]{1,0,2:T(8,128)}, f32[16,65,134]{1,0,2:T(8,128)}, f32[16,65,134]{1,0,2:T(8,128)}) fusion(f32[16,72,136]{1,0,2:T(8,128)} %bitcast.6), kind=kLoop, calls=%fused_computation.184 | loop fusion | flops 975520 | bytes 3344640 | tf_op jit(solution)/shard_map/slice | solution.py:70
  81.9 2.7 %copy.102 = f32[17,64,128]{1,0,2:T(8,128)} copy(f32[17,64,128]{2,1,0:T(8,128)} %get-tuple-element.34) | data formatting | bytes 1114112 | tf_op jit(solution)/shard_map/concatenate | solution.py:64
  84.6 2.7 %copy.103 = f32[17,64,128]{1,0,2:T(8,128)} copy(f32[17,64,128]{2,1,0:T(8,128)} %get-tuple-element.35) | data formatting | bytes 1114112 | tf_op jit(solution)/shard_map/mul | solution.py:42
  87.3 2.8 %copy.104 = f32[17,64,128]{1,0,2:T(8,128)} copy(f32[17,64,128]{2,1,0:T(8,128)} %get-tuple-element.36) | data formatting | bytes 1114112 | tf_op jit(solution)/shard_map/sub | solution.py:42
  90.1 2.7 %copy.105 = f32[17,64,128]{1,0,2:T(8,128)} copy(f32[17,64,128]{2,1,0:T(8,128)} %get-tuple-element.37) | data formatting | bytes 1114112 | tf_op jit(solution)/shard_map/mul | solution.py:43
  92.8 2.7 %copy.106 = f32[17,64,128]{1,0,2:T(8,128)} copy(f32[17,64,128]{2,1,0:T(8,128)} %get-tuple-element.38) | data formatting | bytes 1114112 | tf_op jit(solution)/shard_map/sub | solution.py:43
  95.5 5.7 %fusion.64 = f32[2,16,65,134]{2,1,3,0:T(8,128)S(1)} fusion(f32[2,16,70,134]{2,1,3,0:T(8,128)S(1)} %pad_maximum_fusion.15, f32[2,16,67,134]{2,1,3,0:T(8,128)} %fusion.72, f32[16,65,134]{1,0,2:T(8,128)} %get-tuple-element.31, f32[16,65,134]{1,0,2:T(8,128)} %get-tuple-element.30, f32[16,65,134]{1,0,2:T(8,128)} %get-tuple-element.29, ...), kind=kLoop, calls=%fused_computation.90 | loop fusion | flops 5853120 | bytes 9615840 | tf_op jit(solution)/shard_map/jit(_where)/select_n | solution.py:44
  107.5 2.9 %fusion.8 = f32[2,19,64,128]{2,1,3,0:T(8,128)S(1)} fusion(f32[2,1,64,128]{2,1,3,0:T(1,128)S(1)} %get-tuple-element.16, f32[2,1,64,128]{2,1,3,0:T(1,128)S(1)} %get-tuple-element.17, f32[2,16,64,128]{2,1,3,0:T(8,128)S(1)} %fusion.109), kind=kLoop, calls=%fused_computation.23 | loop fusion | flops 4980736 | bytes 2424832 | tf_op jit(solution)/shard_map/div | solution.py:28
  110.4 3.9 %fusion.18 = f32[2,17,64,128]{2,1,3,0:T(8,128)S(1)} fusion(f32[2,16,64,128]{2,1,3,0:T(8,128)S(1)} %fusion.109, f32[2,1,64,128]{2,1,3,0:T(1,128)S(1)} %get-tuple-element.17, f32[2,1,64,128]{2,1,3,0:T(1,128)S(1)} %get-tuple-element.16, f32[2,19,64,128]{2,1,3,0:T(8,128)S(1)} %fusion.8, f32[17,64,128]{1,0,2:T(8,128)S(1)} %copy-done.11, ...), kind=kLoop, calls=%fused_computation.34 | loop fusion | flops 6406144 | bytes 8560640 | tf_op jit(solution)/shard_map/jit(_where)/select_n | solution.py:44
  114.7 2.7 %fusion.112 = (f32[2,16,3,128]{2,1,3,0:T(8,128)}, f32[2,16,3,128]{2,1,3,0:T(8,128)}) fusion(f32[2,16,64,128]{2,1,3,0:T(8,128)S(1)} %fusion.108), kind=kLoop, calls=%fused_computation.179 | loop fusion | bytes 196608 | tf_op jit(solution)/shard_map/slice | solution.py:14
  117.3 2.4 %copy.107 = f32[2,16,3,128]{3,1,2,0:T(8,128)S(1)} copy(f32[2,16,3,128]{2,1,3,0:T(8,128)} %get-tuple-element.14) | data formatting | bytes 98304 | tf_op jit(solution)/shard_map/slice | solution.py:14
  131.0 3.8 %collective-permute-start.11 = (f32[2,16,70,3]{2,1,3,0:T(8,128)S(1)}, f32[2,16,70,3]{2,1,3,0:T(8,128)S(1)}, u32[]{:S(2)}, u32[]{:S(2)}) collective-permute-start(f32[2,16,70,3]{2,1,3,0:T(8,128)S(1)} %get-tuple-element.6), channel_id=1, source_target_pairs={{1,0},{2,1},{3,2},{0,3},{5,4},{6,5},{7,6},{4,7},{9,8},{10,9},{11,1... | collective-permute-start | bytes 80648 | tf_op jit(solution)/shard_map/ppermute | solution.py:16
  140.3 2.5 %fusion.47 = f32[2,16,65,134]{2,1,3,0:T(8,128)S(1)} fusion(f32[2,16,70,134]{2,1,3,0:T(8,128)S(1)} %pad_maximum_fusion.16, f32[2,16,67,134]{2,1,3,0:T(8,128)S(1)} %fusion.55, f32[16,65,134]{1,0,2:T(8,128)S(1)} %copy-done.16, f32[16,65,134]{1,0,2:T(8,128)S(1)} %copy-done.15, f32[16,65,134]{1,0,2:T(8,128)S(1)} %copy-done.14, f32[16,65,134]{1,0,2:T(8,128)S(1)} %copy-done.13, ...), kind=kLoop, calls=%fused_computation.68 | loop fusion | flops 5853120 | bytes 9615840 | tf_op jit(solution)/shard_map/jit(_where)/select_n | solution.py:44
  148.7 2.9 %fusion.3 = f32[2,19,64,128]{2,1,3,0:T(8,128)S(1)} fusion(f32[2,1,64,128]{2,1,3,0:T(1,128)S(1)} %get-tuple-element.12, f32[2,1,64,128]{2,1,3,0:T(1,128)S(1)} %get-tuple-element.13, f32[2,16,64,128]{2,1,3,0:T(8,128)S(1)} %fusion.107), kind=kLoop, calls=%fused_computation.18 | loop fusion | flops 4980736 | bytes 2424832 | tf_op jit(solution)/shard_map/div | solution.py:28
  151.7 3.7 %fusion.33 = f32[2,17,64,128]{2,1,3,0:T(8,128)S(1)} fusion(f32[2,16,64,128]{2,1,3,0:T(8,128)S(1)} %fusion.107, f32[2,1,64,128]{2,1,3,0:T(1,128)S(1)} %get-tuple-element.13, f32[2,1,64,128]{2,1,3,0:T(1,128)S(1)} %get-tuple-element.12, f32[2,19,64,128]{2,1,3,0:T(8,128)S(1)} %fusion.3, f32[17,64,128]{1,0,2:T(8,128)S(1)} %copy-done.12, ...), kind=kLoop, calls=%fused_computation.51 | loop fusion | flops 6406144 | bytes 8560640 | tf_op jit(solution)/shard_map/jit(_where)/select_n | solution.py:44
  (135 shorter events, 69.5 us)
Async XLA Ops:
  6.5 6.1 %copy-start.34 = (f32[2,16,64,128]{3,2,1,0:T(8,128)S(1)}, f32[2,16,64,128]{3,2,1,0:T(8,128)}, u32[]{:S(2)}) copy-start(f32[2,16,64,128]{3,2,1,0:T(8,128)} %param.4) | copy-start | bytes 3145732
  6.5 24.8 %all-gather.2.cloned.1.call-start = ((), (), s32[]{:S(2)}) async-start(), calls=%async_computation | async-start | bytes 1966080 | tf_op jit(solution)/shard_map/all_gather | solution.py:102
  9.5 5.1 %collective-permute-start = (f32[2,16,3,128]{3,1,2,0:T(8,128)S(1)}, f32[2,16,3,128]{3,1,2,0:T(8,128)S(1)}, u32[]{:S(2)}, u32[]{:S(2)}) collective-permute-start(f32[2,16,3,128]{3,1,2,0:T(8,128)S(1)} %copy.112), channel_id=1, source_target_pairs={{0,4},{4,0},{1,5},{5,1},{2,6},{6,2},{3,7},{7,3},{8,12},{12,8},{9,1... | collective-permute-start | bytes 147464 | tf_op jit(solution)/shard_map/ppermute | solution.py:13
  12.5 4.2 %collective-permute-start.1 = (f32[2,16,3,128]{3,1,2,0:T(8,128)S(1)}, f32[2,16,3,128]{3,1,2,0:T(8,128)S(1)}, u32[]{:S(2)}, u32[]{:S(2)}) collective-permute-start(f32[2,16,3,128]{3,1,2,0:T(8,128)S(1)} %copy.113), channel_id=1, source_target_pairs={{4,0},{0,4},{5,1},{1,5},{6,2},{2,6},{7,3},{3,7},{12,8},{8,12},{13,... | collective-permute-start | bytes 147464 | tf_op jit(solution)/shard_map/ppermute | solution.py:16
  13.5 6.4 %copy-start = (f32[2,16,64,128]{2,1,3,0:T(8,128)}, f32[2,16,64,128]{2,1,3,0:T(8,128)S(1)}, u32[]{:S(2)}) copy-start(f32[2,16,64,128]{2,1,3,0:T(8,128)S(1)} %copy.93) | copy-start | bytes 3145732
  19.9 14.6 %collective-permute-start.2 = (f32[2,16,70,3]{2,1,3,0:T(8,128)S(1)}, f32[2,16,70,3]{2,1,3,0:T(8,128)S(1)}, u32[]{:S(2)}, u32[]{:S(2)}) collective-permute-start(f32[2,16,70,3]{2,1,3,0:T(8,128)S(1)} %get-tuple-element.7), channel_id=1, source_target_pairs={{0,1},{1,2},{2,3},{3,0},{4,5},{5,6},{6,7},{7,4},{8,9},{9,10},{10,1... | collective-permute-start | bytes 80648 | tf_op jit(solution)/shard_map/ppermute | solution.py:13
  22.4 12.1 %collective-permute-start.3 = (f32[2,16,70,3]{2,1,3,0:T(8,128)S(1)}, f32[2,16,70,3]{2,1,3,0:T(8,128)S(1)}, u32[]{:S(2)}, u32[]{:S(2)}) collective-permute-start(f32[2,16,70,3]{2,1,3,0:T(8,128)S(1)} %get-tuple-element.8), channel_id=1, source_target_pairs={{1,0},{2,1},{3,2},{0,3},{5,4},{6,5},{7,6},{4,7},{9,8},{10,9},{11,1... | collective-permute-start | bytes 80648 | tf_op jit(solution)/shard_map/ppermute | solution.py:16
  32.4 6.1 %collective-permute-start.4 = (f32[48,4,128]{2,1,0:T(4,128)S(1)}, f32[48,4,128]{2,1,0:T(4,128)S(1)}, u32[]{:S(2)}, u32[]{:S(2)}) collective-permute-start(f32[48,4,128]{2,1,0:T(4,128)S(1)} %get-tuple-element.20), channel_id=1, source_target_pairs={{0,4},{4,0},{1,5},{5,1},{2,6},{6,2},{3,7},{7,3},{8,12},{12,8},{9,1... | collective-permute-start | bytes 294920 | tf_op jit(solution)/shard_map/ppermute | solution.py:13
  33.9 5.6 %copy-start.28 = (f32[48,64,128]{2,1,0:T(8,128)S(1)}, f32[48,64,128]{2,1,0:T(8,128)}, u32[]{:S(2)}) copy-start(f32[48,64,128]{2,1,0:T(8,128)} %all-gather.2.cloned.1.call-done) | copy-start | bytes 4718596
  33.9 5.6 %collective-permute-start.5 = (f32[48,4,128]{2,1,0:T(4,128)S(1)}, f32[48,4,128]{2,1,0:T(4,128)S(1)}, u32[]{:S(2)}, u32[]{:S(2)}) collective-permute-start(f32[48,4,128]{2,1,0:T(4,128)S(1)} %get-tuple-element.21), channel_id=1, source_target_pairs={{4,0},{0,4},{5,1},{1,5},{6,2},{2,6},{7,3},{3,7},{12,8},{8,12},{13,... | collective-permute-start | bytes 294920 | tf_op jit(solution)/shard_map/ppermute | solution.py:16
  46.1 11.7 %collective-permute-start.7 = (f32[48,72,4]{1,0,2:T(8,128)S(1)}, f32[48,72,4]{1,0,2:T(8,128)S(1)}, u32[]{:S(2)}, u32[]{:S(2)}) collective-permute-start(f32[48,72,4]{1,0,2:T(8,128)S(1)} %copy.96), channel_id=1, source_target_pairs={{1,0},{2,1},{3,2},{0,3},{5,4},{6,5},{7,6},{4,7},{9,8},{10,9},{11,1... | collective-permute-start | bytes 165896 | tf_op jit(solution)/shard_map/ppermute | solution.py:16
  49.5 6.4 %collective-permute-start.6 = (f32[48,72,4]{1,0,2:T(8,128)S(1)}, f32[48,72,4]{1,0,2:T(8,128)S(1)}, u32[]{:S(2)}, u32[]{:S(2)}) collective-permute-start(f32[48,72,4]{1,0,2:T(8,128)S(1)} %copy.95), channel_id=1, source_target_pairs={{0,1},{1,2},{2,3},{3,0},{4,5},{5,6},{6,7},{7,4},{8,9},{9,10},{10,1... | collective-permute-start | bytes 165896 | tf_op jit(solution)/shard_map/ppermute | solution.py:13
  106.9 3.5 %copy-start.9 = (f32[17,64,128]{1,0,2:T(8,128)S(1)}, f32[17,64,128]{1,0,2:T(8,128)}, u32[]{:S(2)}) copy-start(f32[17,64,128]{1,0,2:T(8,128)} %copy.105) | copy-start | bytes 1671172
  106.9 3.5 %copy-start.11 = (f32[17,64,128]{1,0,2:T(8,128)S(1)}, f32[17,64,128]{1,0,2:T(8,128)}, u32[]{:S(2)}) copy-start(f32[17,64,128]{1,0,2:T(8,128)} %copy.106) | copy-start | bytes 1671172
  107.4 3.0 %copy-start.3 = (f32[17,64,128]{1,0,2:T(8,128)S(1)}, f32[17,64,128]{1,0,2:T(8,128)}, u32[]{:S(2)}) copy-start(f32[17,64,128]{1,0,2:T(8,128)} %copy.102) | copy-start | bytes 1671172
  107.4 3.0 %copy-start.5 = (f32[17,64,128]{1,0,2:T(8,128)S(1)}, f32[17,64,128]{1,0,2:T(8,128)}, u32[]{:S(2)}) copy-start(f32[17,64,128]{1,0,2:T(8,128)} %copy.103) | copy-start | bytes 1671172
  119.7 4.4 %collective-permute-start.8 = (f32[2,16,3,128]{3,1,2,0:T(8,128)S(1)}, f32[2,16,3,128]{3,1,2,0:T(8,128)S(1)}, u32[]{:S(2)}, u32[]{:S(2)}) collective-permute-start(f32[2,16,3,128]{3,1,2,0:T(8,128)S(1)} %copy.107), channel_id=1, source_target_pairs={{0,4},{4,0},{1,5},{5,1},{2,6},{6,2},{3,7},{7,3},{8,12},{12,8},{9,1... | collective-permute-start | bytes 147464 | tf_op jit(solution)/shard_map/ppermute | solution.py:13
  123.5 4.1 %collective-permute-start.9 = (f32[2,16,3,128]{3,1,2,0:T(8,128)S(1)}, f32[2,16,3,128]{3,1,2,0:T(8,128)S(1)}, u32[]{:S(2)}, u32[]{:S(2)}) collective-permute-start(f32[2,16,3,128]{3,1,2,0:T(8,128)S(1)} %copy.108), channel_id=1, source_target_pairs={{4,0},{0,4},{5,1},{1,5},{6,2},{2,6},{7,3},{3,7},{12,8},{8,12},{13,... | collective-permute-start | bytes 147464 | tf_op jit(solution)/shard_map/ppermute | solution.py:16
  129.8 7.1 %copy-start.1 = (f32[2,16,3,128]{2,1,3,0:T(8,128)S(1)}, f32[2,16,3,128]{2,1,3,0:T(8,128)}, u32[]{:S(2)}) copy-start(f32[2,16,3,128]{2,1,3,0:T(8,128)} %copy.109) | copy-start | bytes 147460
  129.8 7.1 %copy-start.2 = (f32[2,16,3,128]{2,1,3,0:T(8,128)S(1)}, f32[2,16,3,128]{2,1,3,0:T(8,128)}, u32[]{:S(2)}) copy-start(f32[2,16,3,128]{2,1,3,0:T(8,128)} %copy.110) | copy-start | bytes 147460
  130.9 5.9 %collective-permute-start.10 = (f32[2,16,70,3]{2,1,3,0:T(8,128)S(1)}, f32[2,16,70,3]{2,1,3,0:T(8,128)S(1)}, u32[]{:S(2)}, u32[]{:S(2)}) collective-permute-start(f32[2,16,70,3]{2,1,3,0:T(8,128)S(1)} %get-tuple-element.5), channel_id=1, source_target_pairs={{0,1},{1,2},{2,3},{3,0},{4,5},{5,6},{6,7},{7,4},{8,9},{9,10},{10,1... | collective-permute-start | bytes 80648 | tf_op jit(solution)/shard_map/ppermute | solution.py:13
  131.0 5.9 %collective-permute-start.11 = (f32[2,16,70,3]{2,1,3,0:T(8,128)S(1)}, f32[2,16,70,3]{2,1,3,0:T(8,128)S(1)}, u32[]{:S(2)}, u32[]{:S(2)}) collective-permute-start(f32[2,16,70,3]{2,1,3,0:T(8,128)S(1)} %get-tuple-element.6), channel_id=1, source_target_pairs={{1,0},{2,1},{3,2},{0,3},{5,4},{6,5},{7,6},{4,7},{9,8},{10,9},{11,1... | collective-permute-start | bytes 80648 | tf_op jit(solution)/shard_map/ppermute | solution.py:16
  148.2 3.5 %copy-start.10 = (f32[17,64,128]{1,0,2:T(8,128)S(1)}, f32[17,64,128]{1,0,2:T(8,128)}, u32[]{:S(2)}) copy-start(f32[17,64,128]{1,0,2:T(8,128)} %copy.105) | copy-start | bytes 1671172
  148.2 3.5 %copy-start.12 = (f32[17,64,128]{1,0,2:T(8,128)S(1)}, f32[17,64,128]{1,0,2:T(8,128)}, u32[]{:S(2)}) copy-start(f32[17,64,128]{1,0,2:T(8,128)} %copy.106) | copy-start | bytes 1671172
  (24 other events, 52.3 us)
Sparse Core Ops, SparseCore 0:
  8.9 22.3 all-gather.1
where the time goes:
time: 165 us; the launch traced here: 164 us
  other arithmetic  58.3 us (35%)
  local copies, waits for them, and re-layouts  57.2 us (35%)
  starting transfers between devices  19.1 us (12%)
  waiting for transfers between devices  15.6 us (9%)
  between operations  14 us (8%)
    select_n x6, other arithmetic, advect(): face_flux = jnp.where(faces > 0, from_lower, from_upper)  19.3 us
    slice x6, local copies, waits for them, and re-layouts, extended_2(): lax.slice_in_dim(block, block.shape[dim] - width, None, axis=dim)  11.4 us
    div x6, other arithmetic, advect(): (7.0 * (along(field, 1, cells + 4) + along(field, 2, cells + 5)) - (along...  11.4 us
    ppermute x6, starting transfers between devices, extended_2(): lax.ppermute(lax.slice_in_dim(block, 0, width, axis=dim), axis, backward)  10.5 us
    concatenate x4, other arithmetic, extended_2(): block = jnp.concatenate([low, block, high], axis=dim)  9.52 us
    ppermute x6, starting transfers between devices, extended_2(): lax.ppermute(lax.slice_in_dim(block, block.shape[dim] - width, None, axis...  8.63 us
    all_gather x1, waiting for transfers between devices, gathered(): return lax.all_gather(stacked, 'member', axis=0, tiled=True)  6.81 us
    unnamed x73, local copies, waits for them, and re-layouts  6.71 us
  transfers between devices with their start and end apart: 13, of which 6 were waited for; matrix products, arithmetic and copies ran while one was open for 13% of the time, Pallas kernels for 0%

commit v1 on v0

v1 whole, which is shorter than its diff:
```python
import functools

import jax
import jax.numpy as jnp
from jax import lax
from jax.experimental import pallas as pl
from jax.experimental.pallas import tpu as pltpu
from jax.sharding import PartitionSpec as P

MESH = pl.DeviceIdType.MESH
LANES = 128
GROUP = 8


def lane_roll(x, shift):
    return pltpu.roll(x, shift % LANES, 1)


def coefficients(c):
    s = jnp.abs(c)
    t = 1.0 - s
    ct = c * t * (1.0 / 12.0)
    return c > 0, ct * t, ct * s, c * s * (3.0 - 2.0 * s)


def flux(coefs, e, o, upwind):
    _, near, far, mean = coefs
    return near * e - far * o + mean * upwind


def lane_advect(q, coefs):
    positive = coefs[0]
    below = lane_roll(q, 1)
    p = below + q
    e = 8.0 * p - (lane_roll(p, 1) + lane_roll(p, -1))
    o = jnp.where(positive, lane_roll(e, 1), lane_roll(e, -1))
    f = flux(coefs, e, o, jnp.where(positive, below, q))
    return q - (lane_roll(f, -1) - f)


def kernel(
    sizes,
    tracers,
    flux_x,
    flux_y,
    flux_z,
    out,
    field0,
    field1,
    mid,
    fx,
    fy,
    fz,
    x_edge,
    y_edge,
    x_send,
    y_send,
    own_pack,
    to_right,
    to_left,
    from_left,
    from_right,
    face_left,
    face_right,
    face_flux,
    local_sem,
    wind_send,
    wind_recv,
    edge_send,
    edge_recv,
    halo_send,
    halo_recv,
    pack_send,
    pack_recv,
):
    members, n_x, n_y = sizes
    trac, levels, width_x, width_y = tracers.shape
    slab = levels // members
    groups = width_x // GROUP
    m = lax.axis_index("member")
    ix = lax.axis_index("gx")
    iy = lax.axis_index("gy")

    def member_of(j):
        if j == 0:
            return m
        if j == 1:
            return m + 1 - 2 * lax.rem(m, 2)
        if j == 2:
            return lax.rem(m + 2, 4)
        return 3 - m

    def device(j, dx, dy):
        return (member_of(j), lax.rem(ix + dx + n_x, n_x), lax.rem(iy + dy + n_y, n_y))

    x_steps = (1,) if n_x == 2 else (1, -1)
    y_steps = (1,) if n_y == 2 else (1, -1)
    partners = [(1, 0, 0), (2, 0, 0)]
    partners += [(j, d, 0) for j in range(4) for d in x_steps]
    partners += [(j, 0, d) for j in range(4) for d in y_steps]
    barrier = pltpu.get_barrier_semaphore()
    for partner in partners:
        pl.semaphore_signal(barrier, inc=1, device_id=device(*partner), device_id_type=MESH)

    def levels_of(j):
        return pl.ds(member_of(j) * slab, slab)

    inner = pl.ds(GROUP, width_x)
    winds = ((flux_x, fx), (flux_y, fy), (flux_z, fz))

    def wind_dst(k, j):
        if k == 0:
            return fx.at[levels_of(j), inner, :]
        return winds[k][1].at[levels_of(j), :, :]

    locals_ = [
        pltpu.make_async_copy(winds[k][0], wind_dst(k, 0), local_sem.at[k]) for k in range(3)
    ]
    load = pltpu.make_async_copy(tracers, field0.at[:, :, inner, :], local_sem.at[3])
    locals_[0].start()
    locals_[1].start()
    load.start()
    locals_[2].start()
    pl.semaphore_wait(barrier, len(partners))

    def remote(src, dst, send, recv, dev):
        return pltpu.make_async_remote_copy(
            src_ref=src, dst_ref=dst, send_sem=send, recv_sem=recv, device_id=dev, device_id_type=MESH
        )

    def halo_copies(step, j):
        target = (field0, field1)[step]
        ls = levels_of(j)
        if step == 0:
            low_src = tracers.at[:, ls, pl.ds(0, GROUP), :]
            high_src = tracers.at[:, ls, pl.ds(width_x - GROUP, GROUP), :]
        else:
            low_src = field1.at[:, ls, pl.ds(GROUP, GROUP), :]
            high_src = field1.at[:, ls, pl.ds(width_x, GROUP), :]
        return (
            remote(
                high_src,
                target.at[:, ls, pl.ds(0, GROUP), :],
                halo_send.at[step, j, 0],
                halo_recv.at[step, j, 0],
                device(0, 1, 0),
            ),
            remote(
                low_src,
                target.at[:, ls, pl.ds(width_x + GROUP, GROUP), :],
                halo_send.at[step, j, 1],
                halo_recv.at[step, j, 1],
                device(0, -1, 0),
            ),
        )

    halos = [[halo_copies(step, j) for j in range(4)] for step in range(2)]
    direct = [[remote(winds[k][0], wind_dst(k, 0), wind_send.at[j - 1, k], wind_recv.at[j - 1, k], device(j, 0, 0))
               for k in range(3)] for j in (1, 2)]
    relay = [
        remote(wind_dst(k, 2), wind_dst(k, 2), wind_send.at[2, k], wind_recv.at[2, k], device(1, 0, 0))
        for k in range(3)
    ]
    for j in range(4):
        for c in halos[0][j]:
            c.start()
    for k in range(3):
        direct[1][k].start()
        direct[0][k].start()

    lane = lax.broadcasted_iota(jnp.int32, (GROUP, LANES), 1)
    window = lax.rem(lane, 16)
    low_half = window < 8
    at_edge = (lane < 3) | (lane >= LANES - 3)

    def in_window(g):
        return (lane >= 16 * g) & (lane < 16 * g + 16)

    def packed(pieces):
        total = lane_roll(pieces[0], 8)
        for g in range(1, groups):
            total = jnp.where(in_window(g), lane_roll(pieces[g], 8 + 16 * g), total)
        return total

    locals_[0].wait()
    locals_[1].wait()
    column = jnp.zeros((GROUP, LANES), jnp.float32)
    for k in range(slab):
        x_send[pl.ds(k, 1), :] = fx[m * slab + k, pl.ds(width_x + GROUP - 1, 1), :]
        piece = packed([fy[m * slab + k, pl.ds(GROUP * g, GROUP), :] for g in range(groups)])
        column = jnp.where(window == 4 + k, lane_roll(piece, k - 3), column)
    y_send[...] = column
    edges = []
    for j in range(4):
        edges.append(remote(x_send, x_edge.at[m], edge_send.at[0, j], edge_recv.at[0, j], device(j, 1, 0)))
        edges.append(remote(y_send, y_edge.at[m], edge_send.at[1, j], edge_recv.at[1, j], device(j, 0, 1)))
    for c in edges:
        c.start()

    def wait_edge(axis, j):
        edges[2 * j + axis].wait_recv()

    def wait_wind(k, j):
        if j == 0:
            if k == 2:
                locals_[2].wait()
        elif j == 3:
            relay[k].wait_recv()
        else:
            direct[j - 1][k].wait_recv()

    def pack_copies(step, j):
        ls = levels_of(j)
        return (
            remote(
                to_right.at[step, ls],
                from_left.at[step, ls],
                pack_send.at[step, j, 0],
                pack_recv.at[step, j, 0],
                device(0, 0, 1),
            ),
            remote(
                to_left.at[step, ls],
                from_right.at[step, ls],
                pack_send.at[step, j, 1],
                pack_recv.at[step, j, 1],
                device(0, 0, -1),
            ),
        )

    packs = [[pack_copies(step, j) for j in range(4)] for step in range(2)]

    def sweep_x(step, j):
        field = (field0, field1)[step]
        first = member_of(j) * slab

        def one_level(k, carry):
            level = first + k
            for start in [GROUP * g for g in range(groups)] + [width_x - GROUP + 1]:
                coefs = coefficients(fx[level, pl.ds(GROUP - 1 + start, GROUP), :])
                positive = coefs[0]
                for t in range(trac):
                    q = [field[t, level, pl.ds(GROUP + start + s, GROUP), :] for s in range(-3, 3)]
                    p = [q[i] + q[i + 1] for i in range(5)]
                    e = 8.0 * p[2] - (p[1] + p[3])
                    o = 8.0 * jnp.where(positive, p[1], p[3]) - (jnp.where(positive, p[0], p[4]) + p[2])
                    face_flux[t, pl.ds(start, GROUP), :] = flux(coefs, e, o, jnp.where(positive, q[2], q[3]))
            packs_here = []
            for t in range(trac):
                pieces = []
                for g in range(groups):
                    new = field[t, level, pl.ds(GROUP + GROUP * g, GROUP), :] - (
                        face_flux[t, pl.ds(GROUP * g + 1, GROUP), :] - face_flux[t, pl.ds(GROUP * g, GROUP), :]
                    )
                    mid[t, level, pl.ds(GROUP * g, GROUP), :] = new
                    pieces.append(new)
                both = packed(pieces)
                own_pack[t, level] = both
                packs_here.append(both)
            to_right[step, level] = jnp.where(low_half, packs_here[0], lane_roll(packs_here[1], 8))
            to_left[step, level] = jnp.where(low_half, lane_roll(packs_here[1], -8), packs_here[0])
            return carry

        lax.fori_loop(0, slab, one_level, 0)

    def sweep_y(step, j):
        first = member_of(j) * slab

        def one_level(k, carry):
            level = first + k
            if step == 0:
                rows = [fy[level, pl.ds(GROUP * g, GROUP), :] for g in range(groups)]
                right = lane_roll(packed(rows), 1)
                outer = pltpu.roll(y_edge[member_of(j)], 4 - k, 1)
                left = jnp.where(window == 8, outer, right)
                face_left[level] = left
                face_right[level] = right
            else:
                left = face_left[level]
                right = face_right[level]
            left = coefficients(left)
            right = coefficients(right)
            left_in = from_left[step, level]
            right_in = from_right[step, level]
            fixed = []
            for t in range(trac):
                own = own_pack[t, level]
                lower = left_in if t == 0 else lane_roll(left_in, -8)
                upper = right_in if t == 0 else lane_roll(right_in, 8)
                at_left = lane_advect(jnp.where(low_half, lower, own), left)
                at_right = lane_advect(jnp.where(low_half, own, upper), right)
                fixed.append(jnp.where(low_half, at_right, at_left))
            for g in range(groups):
                coefs = coefficients(lane_roll(fy[level, pl.ds(GROUP * g, GROUP), :], 1))
                for t in range(trac):
                    new = lane_advect(mid[t, level, pl.ds(GROUP * g, GROUP), :], coefs)
                    mid[t, level, pl.ds(GROUP * g, GROUP), :] = jnp.where(
                        at_edge, lane_roll(fixed[t], -(8 + 16 * g)), new
                    )
            return carry

        lax.fori_loop(0, slab, one_level, 0)

    def sweep_z(step, row):
        q = {}
        p = {}
        e = {}
        before = {}

        def cell(t, l):
            l = min(max(l, 0), levels - 1)
            if (t, l) not in q:
                q[t, l] = mid[t, l, pl.ds(row, GROUP), :]
            return q[t, l]

        def pair(t, l):
            if (t, l) not in p:
                p[t, l] = cell(t, l - 1) + cell(t, l)
            return p[t, l]

        def edge(t, l):
            if (t, l) not in e:
                e[t, l] = 8.0 * pair(t, l) - (pair(t, l - 1) + pair(t, l + 1))
            return e[t, l]

        for l in range(levels):
            if l + 1 < levels:
                coefs = coefficients(fz[l, pl.ds(row, GROUP), :])
            for t in range(trac):
                new = cell(t, l)
                if l > 0:
                    new = new + before[t]
                if l + 1 < levels:
                    positive = coefs[0]
                    o = jnp.where(positive, edge(t, l), edge(t, l + 2))
                    f = flux(coefs, edge(t, l + 1), o, jnp.where(positive, cell(t, l), cell(t, l + 1)))
                    new = new - f
                    before[t] = f
                if step == 0:
                    field1[t, l, pl.ds(GROUP + row, GROUP), :] = new
                else:
                    out[t, l, pl.ds(row, GROUP), :] = new

    def sweep_z_groups(step, start, stop):
        def one_group(g, carry):
            sweep_z(step, pl.multiple_of(g * GROUP, GROUP))
            return carry

        lax.fori_loop(start, stop, one_group, 0)

    def exchange(k):
        direct[1][k].wait_recv()
        relay[k].start()

    load.wait()
    for j in range(4):
        for c in halos[0][j]:
            c.wait_recv()
        if j == 1:
            exchange(0)
        if j != 2:
            wait_wind(0, j)
        wait_edge(0, j)
        source = member_of(j)
        for k in range(slab):
            fx[source * slab + k, pl.ds(GROUP - 1, 1), :] = x_edge[source, pl.ds(k, 1), :]
        sweep_x(0, j)
        for c in packs[0][j]:
            c.start()
    for j in range(4):
        wait_edge(1, j)
        if j == 2:
            exchange(1)
        if j != 2:
            wait_wind(1, j)
        for c in packs[0][j]:
            c.wait_recv()
        sweep_y(0, j)
    exchange(2)
    for j in (0, 1, 3):
        wait_wind(2, j)
    sweep_z(0, 0)
    sweep_z(0, width_x - GROUP)
    for j in range(4):
        for c in halos[1][j]:
            c.start()
    sweep_z_groups(0, 1, groups - 1)

    for j in range(4):
        for c in halos[1][j]:
            c.wait_recv()
        sweep_x(1, j)
        for c in packs[1][j]:
            c.start()
    for j in range(4):
        for c in packs[1][j]:
            c.wait_recv()
        sweep_y(1, j)
    sweep_z_groups(1, 0, groups)

    for step in range(2):
        for j in range(4):
            for c in halos[step][j] + packs[step][j]:
                c.wait_send()
    for c in direct[0] + direct[1] + relay + edges:
        c.wait_send()


def body(sizes, tracers, flux_x, flux_y, flux_z):
    trac, levels, width_x, width_y = tracers.shape[0], tracers.shape[1], tracers.shape[2], tracers.shape[3]
    members = sizes[0]
    packed = pltpu.VMEM((2, levels, GROUP, LANES), jnp.float32)
    return pl.pallas_call(
        functools.partial(kernel, sizes),
        out_shape=jax.ShapeDtypeStruct(tracers.shape, jnp.float32),
        in_specs=[pl.BlockSpec(memory_space=pl.ANY)] * 4,
        out_specs=pl.BlockSpec(memory_space=pltpu.VMEM),
        scratch_shapes=[
            pltpu.VMEM((trac, levels, width_x + 2 * GROUP, width_y), jnp.float32),
            pltpu.VMEM((trac, levels, width_x + 2 * GROUP, width_y), jnp.float32),
            pltpu.VMEM((trac, levels, width_x, width_y), jnp.float32),
            pltpu.VMEM((levels, width_x + GROUP, width_y), jnp.float32),
            pltpu.VMEM((levels, width_x, width_y), jnp.float32),
            pltpu.VMEM((levels, width_x, width_y), jnp.float32),
            pltpu.VMEM((members, GROUP, LANES), jnp.float32),
            pltpu.VMEM((members, GROUP, LANES), jnp.float32),
            pltpu.VMEM((GROUP, LANES), jnp.float32),
            pltpu.VMEM((GROUP, LANES), jnp.float32),
            pltpu.VMEM((trac, levels, GROUP, LANES), jnp.float32),
            packed,
            packed,
            packed,
            packed,
            pltpu.VMEM((levels, GROUP, LANES), jnp.float32),
            pltpu.VMEM((levels, GROUP, LANES), jnp.float32),
            pltpu.VMEM((trac, width_x + GROUP, width_y), jnp.float32),
            pltpu.SemaphoreType.DMA((4,)),
            pltpu.SemaphoreType.DMA((3, 3)),
            pltpu.SemaphoreType.DMA((3, 3)),
            pltpu.SemaphoreType.DMA((2, 4)),
            pltpu.SemaphoreType.DMA((2, 4)),
            pltpu.SemaphoreType.DMA((2, 4, 2)),
            pltpu.SemaphoreType.DMA((2, 4, 2)),
            pltpu.SemaphoreType.DMA((2, 4, 2)),
            pltpu.SemaphoreType.DMA((2, 4, 2)),
        ],
        compiler_params=pltpu.CompilerParams(
            collective_id=0, has_side_effects=True, vmem_limit_bytes=48 * 1024 * 1024
        ),
    )(tracers, flux_x, flux_y, flux_z)


def solution(mesh):
    sizes = (mesh.shape["member"], mesh.shape["gx"], mesh.shape["gy"])
    return jax.shard_map(
        functools.partial(body, sizes),
        mesh=mesh,
        in_specs=(
            P("member", None, "gx", "gy"),
            P("member", "gx", "gy"),
            P("member", "gx", "gy"),
            P("member", "gx", "gy"),
        ),
        out_specs=P("member", None, "gx", "gy"),
        check_vma=False,
    )
```

time: 165 us -> 48.8 us (0.30)
  other arithmetic: 58.3 us -> 0 us
  local copies, waits for them, and re-layouts: 57.2 us -> 4.91 us
  Pallas kernels: 0 us -> 43.6 us
  starting transfers between devices: 19.1 us -> 0 us
  waiting for transfers between devices: 15.6 us -> 0 us
  between operations: 14 us -> 0.01 us
    pallas_call x0 -> x1, Pallas kernels: none -> 43.6 us  [body(): pl.pallas_call(functools.partial(kernel, sizes), out_shape=jax.ShapeDtype...]
    slice x14 -> x0, local copies, waits for them, and re-layouts: 21.6 us -> none  [the longest x6 11.4 us: extended_2(): lax.slice_in_dim(block, block.shape[dim] - width, None, axis=dim)]
    select_n x6 -> x0, other arithmetic: 19.3 us -> none  [advect(): face_flux = jnp.where(faces > 0, from_lower, from_upper)]
    ppermute x12 -> x0, starting transfers between devices: 19.1 us -> none  [the longest x6 10.5 us: extended_2(): lax.ppermute(lax.slice_in_dim(block, 0, width, axis=dim), axis, backward)]
    concatenate x6 -> x0, other arithmetic: 13.1 us -> none  [the longest x4 9.52 us: extended_2(): block = jnp.concatenate([low, block, high], axis=dim)]
    ppermute x6 -> x0, local copies, waits for them, and re-layouts: 12.3 us -> none  [the longest x3 6.15 us: extended_2(): lax.ppermute(lax.slice_in_dim(block, block.shape[dim] - width, None, axis...]
    div x6 -> x0, other arithmetic: 11.4 us -> none  [advect(): (7.0 * (along(field, 1, cells + 4) + along(field, 2, cells + 5)) - (along...]
    ppermute x12 -> x0, waiting for transfers between devices: 8.77 us -> none  [the longest x6 6.39 us: extended_2(): lax.ppermute(lax.slice_in_dim(block, block.shape[dim] - width, None, axis...]
  transfers between devices with their start and end apart: 13 -> 0, of which waited for: 6 -> 0; matrix products, arithmetic and copies ran while one was open for 13% -> 0% of each run, Pallas kernels for 0% -> 0%
where the time goes in v1:
time: 48.8 us; the launch traced here: 48.6 us
  Pallas kernels  43.6 us (89%)
  local copies, waits for them, and re-layouts  4.91 us (10%)
    pallas_call x1, Pallas kernels, body(): pl.pallas_call(functools.partial(kernel, sizes), out_shape=jax.ShapeDtype...  43.6 us
    unnamed x9, local copies, waits for them, and re-layouts  4.91 us

profile of v1, /device:TPU:0, one launch (start us, length us, event | category | flops | bytes accessed | tf_op | source)
XLA Modules:
  0.0 48.6 jit_solution(12104019745118469542)
XLA Ops:
  0.0 0.0 copy-start
  0.0 1.2 %copy-done = f32[2,16,64,128]{3,2,1,0:T(8,128)S(1)} copy-done((f32[2,16,64,128]{3,2,1,0:T(8,128)S(1)}, f32[2,16,64,128]{3,2,1,0:T(8,128)}, u32[]{:S(2)}) %copy-start) | copy-done | bytes 1048600
  1.2 0.0 copy-start.1
  1.2 0.9 %copy-done.1 = f32[4,64,128]{2,1,0:T(8,128)S(1)} copy-done((f32[4,64,128]{2,1,0:T(8,128)S(1)}, f32[4,64,128]{2,1,0:T(8,128)}, u32[]{:S(2)}) %copy-start.1) | copy-done | bytes 131096
  2.1 0.0 copy-start.2
  2.1 0.9 %copy-done.2 = f32[4,64,128]{2,1,0:T(8,128)S(1)} copy-done((f32[4,64,128]{2,1,0:T(8,128)S(1)}, f32[4,64,128]{2,1,0:T(8,128)}, u32[]{:S(2)}) %copy-start.2) | copy-done | bytes 131096
  3.0 0.0 copy-start.3
  3.0 0.9 %copy-done.3 = f32[4,64,128]{2,1,0:T(8,128)S(1)} copy-done((f32[4,64,128]{2,1,0:T(8,128)S(1)}, f32[4,64,128]{2,1,0:T(8,128)}, u32[]{:S(2)}) %copy-start.3) | copy-done | bytes 131096
  3.9 43.6 %shard_map.46 = f32[2,16,64,128]{3,2,1,0:T(8,128)S(1)} custom-call(f32[2,16,64,128]{3,2,1,0:T(8,128)S(1)} %copy-done, f32[4,64,128]{2,1,0:T(8,128)S(1)} %copy-done.1, f32[4,64,128]{2,1,0:T(8,128)S(1)} %copy-done.2, f32[4,64,128]{2,1,0:T(8,128)S(1)} %copy-done.3), custom_call_target="tpu_custom_call" | custom-call | tf_op jit(solution)/shard_map/pallas_call | solution.py:413
  47.6 1.0 %copy.6 = f32[2,16,64,128]{3,2,1,0:T(8,128)} copy(f32[2,16,64,128]{3,2,1,0:T(8,128)S(1)} %shard_map.46) | data formatting | bytes 2097152
Async XLA Ops:
  0.0 1.2 %copy-start = (f32[2,16,64,128]{3,2,1,0:T(8,128)S(1)}, f32[2,16,64,128]{3,2,1,0:T(8,128)}, u32[]{:S(2)}) copy-start(f32[2,16,64,128]{3,2,1,0:T(8,128)} %tracers.1) | copy-start | bytes 3145732
  1.2 0.9 %copy-start.1 = (f32[4,64,128]{2,1,0:T(8,128)S(1)}, f32[4,64,128]{2,1,0:T(8,128)}, u32[]{:S(2)}) copy-start(f32[4,64,128]{2,1,0:T(8,128)} %flux_x.1) | copy-start | bytes 393220
  2.1 0.9 %copy-start.2 = (f32[4,64,128]{2,1,0:T(8,128)S(1)}, f32[4,64,128]{2,1,0:T(8,128)}, u32[]{:S(2)}) copy-start(f32[4,64,128]{2,1,0:T(8,128)} %flux_y.1) | copy-start | bytes 393220
  3.0 0.9 %copy-start.3 = (f32[4,64,128]{2,1,0:T(8,128)S(1)}, f32[4,64,128]{2,1,0:T(8,128)}, u32[]{:S(2)}) copy-start(f32[4,64,128]{2,1,0:T(8,128)} %flux_z.1) | copy-start | bytes 393220

commit v2 on v1

--- a/solution.py
+++ b/solution.py
@@ -10,6 +10,7 @@
 MESH = pl.DeviceIdType.MESH
 LANES = 128
 GROUP = 8
+RIM = 3
 
 
 def lane_roll(x, shift):
@@ -28,14 +29,25 @@
     return near * e - far * o + mean * upwind
 
 
-def lane_advect(q, coefs):
+def lane_advect(q, products, coefs):
+    e, e_below, e_above, below = products
     positive = coefs[0]
-    below = lane_roll(q, 1)
-    p = below + q
-    e = 8.0 * p - (lane_roll(p, 1) + lane_roll(p, -1))
-    o = jnp.where(positive, lane_roll(e, 1), lane_roll(e, -1))
-    f = flux(coefs, e, o, jnp.where(positive, below, q))
+    f = flux(coefs, e, jnp.where(positive, e_below, e_above), jnp.where(positive, below, q))
     return q - (lane_roll(f, -1) - f)
+
+
+def stencil_matrix(shape):
+    cell = lax.rem(lax.broadcasted_iota(jnp.int32, shape, 0), LANES)
+    column = lax.broadcasted_iota(jnp.int32, shape, 1)
+    face = lax.rem(column, LANES)
+    part = column // LANES
+    base = jnp.where(part == 1, -1, jnp.where(part == 2, 1, 0))
+    offset = lax.rem(cell - face - base + 2 * LANES, LANES)
+    edge = jnp.where((offset == 0) | (offset == LANES - 1), 7.0, 0.0) - jnp.where(
+        (offset == 1) | (offset == LANES - 2), 1.0, 0.0
+    )
+    shifted = jnp.where(offset == LANES - 1, 1.0, 0.0)
+    return jnp.where(part == 3, shifted, edge)
 
 
 def kernel(
@@ -63,6 +75,9 @@
     face_left,
     face_right,
     face_flux,
+    stencil,
+    halves,
+    products,
     local_sem,
     wind_send,
     wind_recv,
@@ -121,6 +136,7 @@
     locals_[1].start()
     load.start()
     locals_[2].start()
+    stencil[...] = stencil_matrix(stencil.shape).astype(jnp.bfloat16)
     pl.semaphore_wait(barrier, len(partners))
 
     def remote(src, dst, send, recv, dev):
@@ -132,22 +148,22 @@
         target = (field0, field1)[step]
         ls = levels_of(j)
         if step == 0:
-            low_src = tracers.at[:, ls, pl.ds(0, GROUP), :]
-            high_src = tracers.at[:, ls, pl.ds(width_x - GROUP, GROUP), :]
+            low_src = tracers.at[:, ls, pl.ds(0, RIM), :]
+            high_src = tracers.at[:, ls, pl.ds(width_x - RIM, RIM), :]
         else:
-            low_src = field1.at[:, ls, pl.ds(GROUP, GROUP), :]
-            high_src = field1.at[:, ls, pl.ds(width_x, GROUP), :]
+            low_src = field1.at[:, ls, pl.ds(GROUP, RIM), :]
+            high_src = field1.at[:, ls, pl.ds(GROUP + width_x - RIM, RIM), :]
         return (
             remote(
                 high_src,
-                target.at[:, ls, pl.ds(0, GROUP), :],
+                target.at[:, ls, pl.ds(GROUP - RIM, RIM), :],
                 halo_send.at[step, j, 0],
                 halo_recv.at[step, j, 0],
                 device(0, 1, 0),
             ),
             remote(
                 low_src,
-                target.at[:, ls, pl.ds(width_x + GROUP, GROUP), :],
+                target.at[:, ls, pl.ds(width_x + GROUP, RIM), :],
                 halo_send.at[step, j, 1],
                 halo_recv.at[step, j, 1],
                 device(0, -1, 0),
@@ -263,11 +279,45 @@
 
         lax.fori_loop(0, slab, one_level, 0)
 
+    per_level = trac * (width_x + 2 * GROUP)
+
     def sweep_y(step, j):
         first = member_of(j) * slab
 
+        def put(row, x):
+            high = x.astype(jnp.bfloat16)
+            low = (x - high.astype(jnp.float32)).astype(jnp.bfloat16)
+            rows = pl.ds(pl.multiple_of(row, 16), 16)
+            halves[rows, pl.ds(0, LANES)] = high
+            halves[rows, pl.ds(LANES, LANES)] = low
+
+        def windows(level):
+            left_in = from_left[step, level]
+            right_in = from_right[step, level]
+            result = []
+            for t in range(trac):
+                own = own_pack[t, level]
+                lower = left_in if t == 0 else lane_roll(left_in, -8)
+                upper = right_in if t == 0 else lane_roll(right_in, 8)
+                result.append((jnp.where(low_half, lower, own), jnp.where(low_half, own, upper)))
+            return result
+
+        def split(k, carry):
+            level = first + k
+            start = k * per_level
+            for t in range(trac):
+                for r in range(width_x // 16):
+                    put(start + t * width_x + 16 * r, mid[t, level, pl.ds(16 * r, 16), :])
+            for t, pair in enumerate(windows(level)):
+                put(start + trac * width_x + 16 * t, jnp.concatenate(pair, axis=0))
+            return carry
+
+        lax.fori_loop(0, slab, split, 0)
+        products[...] = jnp.dot(halves[...], stencil[...], preferred_element_type=jnp.float32)
+
         def one_level(k, carry):
             level = first + k
+            start = k * per_level
             if step == 0:
                 rows = [fy[level, pl.ds(GROUP * g, GROUP), :] for g in range(groups)]
                 right = lane_roll(packed(rows), 1)
@@ -280,23 +330,23 @@
                 right = face_right[level]
             left = coefficients(left)
             right = coefficients(right)
-            left_in = from_left[step, level]
-            right_in = from_right[step, level]
+
+            def parts(row):
+                rows = pl.ds(pl.multiple_of(start + row, GROUP), GROUP)
+                return [products[rows, pl.ds(LANES * i, LANES)] for i in range(4)]
+
             fixed = []
-            for t in range(trac):
-                own = own_pack[t, level]
-                lower = left_in if t == 0 else lane_roll(left_in, -8)
-                upper = right_in if t == 0 else lane_roll(right_in, 8)
-                at_left = lane_advect(jnp.where(low_half, lower, own), left)
-                at_right = lane_advect(jnp.where(low_half, own, upper), right)
+            for t, (at_left, at_right) in enumerate(windows(level)):
+                row = trac * width_x + 16 * t
+                at_left = lane_advect(at_left, parts(row), left)
+                at_right = lane_advect(at_right, parts(row + GROUP), right)
                 fixed.append(jnp.where(low_half, at_right, at_left))
             for g in range(groups):
                 coefs = coefficients(lane_roll(fy[level, pl.ds(GROUP * g, GROUP), :], 1))
                 for t in range(trac):
-                    new = lane_advect(mid[t, level, pl.ds(GROUP * g, GROUP), :], coefs)
-                    mid[t, level, pl.ds(GROUP * g, GROUP), :] = jnp.where(
-                        at_edge, lane_roll(fixed[t], -(8 + 16 * g)), new
-                    )
+                    rows = pl.ds(GROUP * g, GROUP)
+                    new = lane_advect(mid[t, level, rows, :], parts(t * width_x + GROUP * g), coefs)
+                    mid[t, level, rows, :] = jnp.where(at_edge, lane_roll(fixed[t], -(8 + 16 * g)), new)
             return carry
 
         lax.fori_loop(0, slab, one_level, 0)
@@ -409,11 +459,12 @@
 def body(sizes, tracers, flux_x, flux_y, flux_z):
     trac, levels, width_x, width_y = tracers.shape[0], tracers.shape[1], tracers.shape[2], tracers.shape[3]
     members = sizes[0]
+    matrix_rows = levels // members * trac * (width_x + 2 * GROUP)
     packed = pltpu.VMEM((2, levels, GROUP, LANES), jnp.float32)
     return pl.pallas_call(
         functools.partial(kernel, sizes),
         out_shape=jax.ShapeDtypeStruct(tracers.shape, jnp.float32),
-        in_specs=[pl.BlockSpec(memory_space=pl.ANY)] * 4,
+        in_specs=[pl.BlockSpec(memory_space=pltpu.HBM)] * 4,
         out_specs=pl.BlockSpec(memory_space=pltpu.VMEM),
         scratch_shapes=[
             pltpu.VMEM((trac, levels, width_x + 2 * GROUP, width_y), jnp.float32),
@@ -434,6 +485,9 @@
             pltpu.VMEM((levels, GROUP, LANES), jnp.float32),
             pltpu.VMEM((levels, GROUP, LANES), jnp.float32),
             pltpu.VMEM((trac, width_x + GROUP, width_y), jnp.float32),
+            pltpu.VMEM((2 * LANES, 4 * LANES), jnp.bfloat16),
+            pltpu.VMEM((matrix_rows, 2 * LANES), jnp.bfloat16),
+            pltpu.VMEM((matrix_rows, 4 * LANES), jnp.float32),
             pltpu.SemaphoreType.DMA((4,)),
             pltpu.SemaphoreType.DMA((3, 3)),
             pltpu.SemaphoreType.DMA((3, 3)),
@@ -445,7 +499,7 @@
             pltpu.SemaphoreType.DMA((2, 4, 2)),
         ],
         compiler_params=pltpu.CompilerParams(
-            collective_id=0, has_side_effects=True, vmem_limit_bytes=48 * 1024 * 1024
+            collective_id=0, has_side_effects=True
         ),
     )(tracers, flux_x, flux_y, flux_z)
 

time: 48.8 us -> 45 us (0.922)
  local copies, waits for them, and re-layouts: 4.91 us -> 2.31 us
  Pallas kernels: 43.6 us -> 42.6 us
    unnamed x9 -> x1, local copies, waits for them, and re-layouts: 4.91 us -> 2.31 us
    pallas_call x1, Pallas kernels: 43.6 us -> 42.6 us  [body(): pl.pallas_call(functools.partial(kernel, sizes), out_shape=jax.ShapeDtype...]
where the time goes in v2:
time: 45 us; the launch traced here: 44.9 us
  Pallas kernels  42.6 us (95%)
  local copies, waits for them, and re-layouts  2.31 us (5%)
    pallas_call x1, Pallas kernels, body(): pl.pallas_call(functools.partial(kernel, sizes), out_shape=jax.ShapeDtype...  42.6 us
    unnamed x1, local copies, waits for them, and re-layouts  2.31 us

profile of v2, /device:TPU:0, one launch (start us, length us, event | category | flops | bytes accessed | tf_op | source)
XLA Modules:
  0.0 44.9 jit_solution(8933282171819754724)
XLA Ops:
  0.0 42.6 %shard_map.46 = f32[2,16,64,128]{3,2,1,0:T(8,128)} custom-call(f32[2,16,64,128]{3,2,1,0:T(8,128)} %tracers.1, f32[4,64,128]{2,1,0:T(8,128)} %flux_x.1, f32[4,64,128]{2,1,0:T(8,128)} %flux_y.1, f32[4,64,128]{2,1,0:T(8,128)} %flux_z.1), custom_call_target="tpu_custom_call" | custom-call | tf_op jit(solution)/shard_map/pallas_call | solution.py:464
  42.6 2.3 %copy.6 = f32[2,16,64,128]{3,2,1,0:T(8,128)} copy(f32[2,16,64,128]{3,2,1,0:T(8,128)} %shard_map.46) | data formatting | bytes 2097152
